TPU v7x, 32 devices: a whole 2x2x4 slice. The times are simulated.
32 devices in a mesh: seq: 8 (over y, x, core), head: 4 (over z).
Axes of the slice: x: 2, y: 2, z: 4, core: 2. Of those that a mesh axis runs over, the one named last changes fastest.
Arguments:
- out_grad: bfloat16 [2048, 4096], P('seq', 'head'), may hold values from -7.2 to 7.2
- x_in: bfloat16 [2048, 4096], P('seq', 'head'), may hold values from -6 to 6
- b_in: bfloat16 [2048, 128], P('seq'), may hold values from -2.5 to 2.5
- c_in: bfloat16 [2048, 128], P('seq'), may hold values from -2.5 to 2.5
- dt_raw: float32 [64, 2048], P('head', 'seq'), may hold values from -5.1 to -0.7
- dt_bias: float32 [64], P('head'), may hold values from -0.5 to 0.5
- a_log: float32 [64], P('head'), may hold values from -7.5 to 2.2
- d_skip: float32 [64], P('head'), may hold values from 0.5 to 1.5
- states: bfloat16 [8, 4096, 128], P('seq', 'head'), may hold values from -6 to 6
- w_out: bfloat16 [4096, 4096], P('head'), may hold values from -0.09375 to 0.09375
- w_in: bfloat16 [4096, 4096], P(None, 'head'), may hold values from -0.125 to 0.125
Outputs:
- in_grad: bfloat16 [4096, 2048], P('head', 'seq')
- bc_grad: bfloat16 [256, 2048], P('head', 'seq')
- dt_grad: float32 [64, 2048], P('head', 'seq')
- param_grad: float32 [3, 64], P(None, 'head')
All inputs are finite; a program needn't handle non-finite values.
Results may differ from a plain program's by a relative error of at most 0.015.
Values may be sent and summed in bfloat16 or wider, within the bound.
A program may use at most 64 MiB of HBM per device.

v0:
```python
import jax
import jax.numpy as jnp
from jax import lax
from jax.sharding import PartitionSpec as P


def entering(value, axis, join, neutral):
    count, mine = (lax.axis_size(axis), lax.axis_index(axis))
    pieces = jax.tree.map(lambda part: lax.all_gather(part, axis), value)
    pieces = jax.tree.map(lambda part: part[::-1], pieces)
    mine = count - 1 - mine
    so_far = jax.tree.map(
        lambda part, zero: jnp.full_like(part, 0) + jnp.asarray(zero, part.dtype), value, neutral
    )

    def turn(position, so_far):
        longer = join(so_far, jax.tree.map(lambda part: part[position], pieces))
        return jax.tree.map(lambda new, old: jnp.where(position < mine, new, old), longer, so_far)

    return lax.fori_loop(0, count - 1, turn, so_far)


def shards(out_grad, x_in, b_in, c_in, dt_raw, dt_bias, a_log, d_skip, states, w_out, w_in):
    tokens_here, inner_here = x_in.shape
    group_heads = dt_raw.shape[0]
    head_dim = inner_here // group_heads
    state_dim = b_in.shape[1]
    contract_last = (((1,), (1,)), ((), ()))
    head_sum = lax.dot_general(
        lax.all_gather(out_grad, "head", axis=1, tiled=True),
        w_out,
        contract_last,
        preferred_element_type=jnp.float32,
    )
    dy_heads = head_sum.astype(jnp.bfloat16).reshape(tokens_here, group_heads, head_dim)
    dy_wide = dy_heads.astype(jnp.float32)
    x_heads = x_in.reshape(tokens_here, group_heads, head_dim)
    x_wide = x_heads.astype(jnp.float32)
    decay_rate = jnp.exp(a_log)
    step_size = jax.nn.softplus(dt_raw + dt_bias[:, None])
    log_step = -decay_rate[:, None] * step_size
    cumlog = jnp.cumsum(log_step, axis=1)
    positions = jnp.arange(tokens_here)
    causal = positions[:, None] >= positions[None, :]
    log_gaps = cumlog[:, :, None] - cumlog[:, None, :]
    decay_mask = jnp.where(causal[None], jnp.exp(jnp.minimum(log_gaps, 0.0)), 0.0)
    scores = lax.dot_general(c_in, b_in, contract_last, preferred_element_type=jnp.float32)
    step_rows = step_size.T
    x_scaled = (x_wide * step_rows[:, :, None]).astype(jnp.bfloat16)
    pair_dots = jnp.einsum("ihp,jhp->hij", dy_heads, x_scaled, preferred_element_type=jnp.float32)
    kernel = (scores[None] * decay_mask).astype(jnp.bfloat16)
    intra_back = jnp.einsum("hij,ihp->jhp", kernel, dy_heads, preferred_element_type=jnp.float32)
    masked_dots = (pair_dots * decay_mask).astype(jnp.bfloat16)
    start_decay = jnp.exp(cumlog)
    dy_decay = (dy_wide * start_decay.T[:, :, None]).astype(jnp.bfloat16)
    local_state = jnp.einsum("ihp,in->hpn", dy_decay, c_in, preferred_element_type=jnp.float32)
    end_total = jnp.exp(cumlog[:, -1])
    entry_state = states.reshape(group_heads, head_dim, state_dim)
    db_intra = jnp.einsum("hij,in->nj", masked_dots, c_in, preferred_element_type=jnp.float32)
    dc_intra = jnp.einsum("hij,jn->ni", masked_dots, b_in, preferred_element_type=jnp.float32)
    dc_entry = jnp.einsum("ihp,hpn->ni", dy_decay, entry_state, preferred_element_type=jnp.float32)
    ystate = jnp.einsum("in,hpn->ihp", c_in, entry_state, preferred_element_type=jnp.float32)
    pair_weight = pair_dots * scores[None] * decay_mask
    state_terms = start_decay * jnp.sum(dy_wide * ystate, axis=2).T
    skip_terms = jnp.sum(dy_wide * x_wide, axis=(0, 2))

    def compose(earlier, nearer):
        return (nearer[0] * earlier[0], nearer[0][:, None, None] * earlier[1] + nearer[1])

    identity_pair = (jnp.ones_like(end_total), jnp.zeros_like(local_state))
    carried = entering((end_total, local_state), "seq", compose, identity_pair)[1]
    carried_bf = carried.astype(jnp.bfloat16)
    state_back = jnp.einsum("jn,hpn->jhp", b_in, carried_bf, preferred_element_type=jnp.float32)
    end_decay = jnp.exp(cumlog[:, -1:] - cumlog)
    end_weight = (step_size * end_decay).T
    x_grad = (
        (
            step_rows[:, :, None] * intra_back
            + end_weight[:, :, None] * state_back
            + d_skip[None, :, None] * dy_wide
        )
        .astype(jnp.bfloat16)
        .reshape(tokens_here, inner_here)
    )
    x_end = (x_wide * end_weight[:, :, None]).astype(jnp.bfloat16)
    db_entry = jnp.einsum("jhp,hpn->nj", x_end, carried_bf, preferred_element_type=jnp.float32)
    bc_part = jnp.concatenate([db_intra + db_entry, dc_intra + dc_entry], axis=0)
    end_terms = end_weight.T * jnp.sum(x_wide * state_back, axis=2).T
    cum_grad = pair_weight.sum(axis=2) - pair_weight.sum(axis=1) + state_terms - end_terms
    tail_grad = end_terms.sum(axis=1) + end_total * jnp.sum(
        entry_state.astype(jnp.float32) * carried, axis=(1, 2)
    )
    cum_grad = cum_grad.at[:, -1].add(tail_grad)
    step_grad = jnp.cumsum(cum_grad[:, ::-1], axis=1)[:, ::-1]
    dt_sum = (
        -decay_rate[:, None] * step_grad
        + jnp.sum(x_wide * (intra_back + end_decay.T[:, :, None] * state_back), axis=2).T
    )
    dt_grad = dt_sum * jax.nn.sigmoid(dt_raw + dt_bias[:, None])
    param_terms = jnp.stack(
        [jnp.sum(step_grad * log_step, axis=1), skip_terms, jnp.sum(dt_grad, axis=1)]
    )
    in_part = lax.psum_scatter(
        lax.dot_general(w_in, x_grad, contract_last, preferred_element_type=jnp.float32).astype(
            jnp.bfloat16
        ),
        "head",
        scatter_dimension=0,
        tiled=True,
    )
    bc_sum = lax.psum_scatter(bc_part.astype(jnp.bfloat16), "head", scatter_dimension=0, tiled=True)
    norm_scale = (lax.axis_size("seq") * tokens_here * head_dim) ** (-0.5)
    param_grad = lax.psum(param_terms, "seq") * norm_scale
    return (in_part, bc_sum, dt_grad, param_grad)


def solution(mesh):
    return jax.shard_map(
        shards,
        mesh=mesh,
        in_specs=(
            P("seq", "head"),
            P("seq", "head"),
            P("seq", None),
            P("seq", None),
            P("head", "seq"),
            P("head"),
            P("head"),
            P("head"),
            P("seq", "head", None),
            P("head", None),
            P(None, "head"),
        ),
        out_specs=(P("head", "seq"), P("head", "seq"), P("head", "seq"), P(None, "head")),
        check_vma=False,
    )
```

profile of v0, /device:TPU:0, one launch (start us, length us, event | category | flops | bytes accessed | tf_op | source)
XLA Modules:
  0.0 200.9 jit_solution(2288571976925971934)
XLA Ops:
  7.2 0.7 all-gather.5.cloned.1.call-update
  8.0 0.7 exponential_negate_fusion
  8.6 0.5 copy-done.22
  9.2 0.8 copy_bitcast_fusion.3
  10.0 0.6 reduce-window.14
  11.0 1.4 fusion.35
  12.6 0.3 copy.72
  12.9 45.1 %all-gather.5.cloned.1.call-done = bf16[256,4096]{1,0:T(8,128)(2,1)} async-done(((bf16[256,1024]{1,0:T(8,128)(2,1)}), bf16[256,4096]{1,0:T(8,128)(2,1)}) %all-gather.5.cloned.1.call-update) | async-done | bytes 2097168 | tf_op jit(solution)/shard_map/all_gather | solution.py:30
  58.0 7.8 %fusion.17 = (f32[1024]{0:T(1024)}, bf16[256,1024]{1,0:T(8,128)(2,1)}, bf16[256,1024]{1,0:T(8,128)(2,1)S(1)}) fusion(bf16[256,1024]{1,0:T(8,128)(2,1)} %param.16, f32[256,1024]{1,0:T(8,128)S(1)} %copy.72, bf16[256,4096]{1,0:T(8,128)(2,1)} %all-gather.5.cloned.1.call-done, bf16[1024,4096]{1,0:T(8,128)(2,1)} %param.24), kind=kOutput, calls=%fused_computation.36 | convolution fusion | flops 2149317632 | bytes 13111296 | tf_op jit(solution)/shard_map/dot_general | solution.py:29
  66.0 1.1 fusion.22
  67.5 0.6 dynamic-slice.8
  68.6 0.2 dynamic-update-slice.3
  68.9 13.9 %all-reduce = f32[128]{0:T(128)S(1)} all-reduce(f32[128]{0:T(128)S(1)} %dynamic-update-slice.3), channel_id=2, replica_groups=mesh['seq'=8,'head'=4] {'seq'}, use_global_device_ids=true, to_apply=%add | all-reduce | flops 128 | bytes 1024
  82.9 0.6 rev.12
  83.7 0.4 copy-done.15
  84.1 2.0 fusion.10
  86.1 16.6 %all-gather.7.cloned.1.call-done = f32[128,64,128]{2,1,0:T(8,128)} async-done(((f32[16,64,128]{2,1,0:T(8,128)}), f32[128,64,128]{2,1,0:T(8,128)}) %all-gather.7.cloned.1.call-update) | async-done | bytes 4194320 | tf_op jit(solution)/shard_map/all_gather | solution.py:9
  102.8 4.7 %rev.13 = f32[8,16,64,128]{3,2,1,0:T(8,128)} reverse(f32[8,16,64,128]{3,2,1,0:T(8,128)} %bitcast.136), dimensions={0} | reverse | bytes 8388608 | tf_op jit(solution)/shard_map/rev | solution.py:10
  107.5 13.2 %while.15 = (s32[]{:T(128)}, f32[16,64,128]{2,1,0:T(8,128)S(1)}, s32[]{:T(128)}, f32[8,16]{1,0:T(8,128)}, f32[8,16,64,128]{3,2,1,0:T(8,128)}, /*index=5*/s32[]{:T(128)}, s32[]{:T(128)}) while((s32[]{:T(128)}, f32[16,64,128]{2,1,0:T(8,128)S(1)}, s32[]{:T(128)}, f32[8,16]{1,0:T(8,128)}, f32[8,16,64,128]{3,2,1,0:T(8,128)}, ...), condition=%wide.region_3.4_spmd.clone, body=%wide.region_2.3_spmd.clone.sunk | while | flops 524292 | bytes 1573161 | solution.py:20
  107.5 0.7 dynamic-slice_bitcast_fusion.2
  108.2 1.2 fusion.62
  109.4 0.7 dynamic-slice_bitcast_fusion.2
  110.1 1.2 fusion.62
  111.3 0.7 dynamic-slice_bitcast_fusion.2
  112.0 1.2 fusion.62
  113.2 0.7 dynamic-slice_bitcast_fusion.2
  113.9 1.2 fusion.62
  115.0 0.7 dynamic-slice_bitcast_fusion.2
  115.7 1.2 fusion.62
  116.9 0.7 dynamic-slice_bitcast_fusion.2
  117.6 1.2 fusion.62
  118.8 0.7 dynamic-slice_bitcast_fusion.2
  119.5 1.2 fusion.62
  120.7 1.2 multiply_reduce_fusion.1
  121.9 7.2 %fusion.1 = bf16[4096,256]{0,1:T(8,128)(2,1)} fusion(bf16[256,1024]{0,1:T(8,128)(2,1)S(1)} %bitcast.142, bf16[4096,1024]{1,0:T(8,128)(2,1)} %param.25), kind=kOutput, calls=%fused_computation.4 | convolution fusion | flops 2148532224 | bytes 11010048 | tf_op jit(solution)/shard_map/dot_general | solution.py:104
  129.3 0.7 reduce_sum.127
  130.3 0.3 convolution_bitcast_fusion.1
  130.5 0.3 fusion.11
  131.0 3.5 %fusion.2 = (f32[16,256]{1,0:T(8,128)S(1)}, f32[16,256]{1,0:T(8,128)S(1)}, bf16[256,256]{1,0:T(8,128)(2,1)S(1)}) fusion(f32[16,256]{1,0:T(8,128)} %copy-done.13, f32[256,256]{1,0:T(8,128)} %copy-done.5, pred[256,256]{1,0:T(8,128)(4,1)} %copy-done.15, bf16[256,16,64]{0,2,1:T(8,128)(2,1)S(1)} %bitcast.135, f32[256,16,64]{0,2,1:T(8,128)S(1)} %bitcast.130, ...), kind=kOutput, calls=%fused_computation.10 | convolution fusion | flops 146202624 | bytes 2097152 | tf_op jit(solution)/shard_map/ihp,jhp->hij/dot_general | solution.py:50
  135.7 0.6 reduce-window.16
  136.7 0.3 convolution_bitcast_fusion.2
  137.2 0.7 pad_maximum_fusion
  137.8 0.8 fusion.42
  138.7 13.9 %psum.7 = f32[3,16]{1,0:T(4,128)S(1)} all-reduce(f32[3,16]{1,0:T(4,128)S(1)} %pad_maximum_fusion.1), channel_id=1, replica_groups=mesh['seq'=8,'head'=4] {'seq'}, use_global_device_ids=true, to_apply=%region_20.21 | all-reduce | flops 48 | bytes 384 | tf_op jit(solution)/shard_map/psum | solution.py:113
  152.6 0.6 broadcast_multiply_fusion
  153.2 19.8 %reduce-scatter.3.cloned.1.call-done = bf16[1024,256]{0,1:T(8,128)(2,1)} async-done(((bf16[4096,256]{0,1:T(8,128)(2,1)}), bf16[1024,256]{0,1:T(8,128)(2,1)}) %reduce-scatter.3.cloned.1.call-update) | async-done | bytes 524304 | tf_op jit(solution)/shard_map/reduce_scatter | solution.py:103
  173.0 2.0 %copy.78 = bf16[1024,256]{1,0:T(8,128)(2,1)} copy(bf16[1024,256]{0,1:T(8,128)(2,1)} %reduce-scatter.3.cloned.1.call-done) | data formatting | bytes 1048576
  175.0 19.4 %reduce-scatter.5.cloned.1.call-done = bf16[64,256]{1,0:T(8,128)(2,1)} async-done(((bf16[256,256]{1,0:T(8,128)(2,1)}), bf16[64,256]{1,0:T(8,128)(2,1)}) %reduce-scatter.5.cloned.1.call-update) | async-done | bytes 32784 | tf_op jit(solution)/shard_map/reduce_scatter | solution.py:111
  (90 shorter events, 3.7 us)
Async XLA Ops:
  7.2 76.3 %copy-start = (bf16[256,128]{1,0:T(8,128)(2,1)S(1)}, bf16[256,128]{1,0:T(8,128)(2,1)}, u32[]{:S(2)}) copy-start(bf16[256,128]{1,0:T(8,128)(2,1)} %param.17) | copy-start | bytes 196612
  7.2 50.8 %all-gather.5.cloned.1.call-start = ((), (), s32[]{:S(2)}) async-start(), calls=%async_computation.2 | async-start | bytes 2621440 | tf_op jit(solution)/shard_map/all_gather | solution.py:30
  7.9 94.9 %all-gather.7.cloned.1.call-start = ((), (), s32[]{:S(2)}) async-start(), calls=%async_computation.5 | async-start | bytes 4718592 | tf_op jit(solution)/shard_map/all_gather | solution.py:9
  8.6 0.5 copy-start.22
  10.8 55.0 %copy-start.16 = (f32[16,2]{0,1:T(2,128)}, f32[16,2]{0,1:T(2,128)S(1)}, u32[]{:S(2)}) copy-start(f32[16,2]{0,1:T(2,128)S(1)} %slice.34) | copy-start | bytes 388
  10.8 1.6 copy-start.13
  11.0 54.8 %copy-start.19 = (f32[16]{0:T(128)}, f32[16]{0:T(128)S(1)}, u32[]{:S(2)}) copy-start(f32[16]{0:T(128)S(1)} %get-tuple-element.154) | copy-start | bytes 196
  12.9 53.1 %copy-start.2 = (bf16[256,128]{1,0:T(8,128)(2,1)S(1)}, bf16[256,128]{1,0:T(8,128)(2,1)}, u32[]{:S(2)}) copy-start(bf16[256,128]{1,0:T(8,128)(2,1)} %param.18) | copy-start | bytes 196612
  12.9 54.3 %copy-start.3 = (bf16[256,1024]{1,0:T(8,128)(2,1)S(1)}, bf16[256,1024]{1,0:T(8,128)(2,1)}, u32[]{:S(2)}) copy-start(bf16[256,1024]{1,0:T(8,128)(2,1)} %param.16) | copy-start | bytes 1572868
  65.8 1.6 copy-start.26
  67.2 105.8 %reduce-scatter.3.cloned.1.call-start = ((), (), s32[]{:S(2)}) async-start(), calls=%async_computation.3 | async-start | bytes 2621440 | tf_op jit(solution)/shard_map/reduce_scatter | solution.py:103
  83.5 0.6 copy-start.15
  84.1 23.4 %copy-start.5 = (f32[256,256]{1,0:T(8,128)}, f32[256,256]{1,0:T(8,128)S(1)}, u32[]{:S(2)}) copy-start(f32[256,256]{1,0:T(8,128)S(1)} %fusion.44) | copy-start | bytes 786436
  107.5 13.2 %copy-start.7 = (f32[256,16]{0,1:T(8,128)S(1)}, f32[256,16]{0,1:T(8,128)}, u32[]{:S(2)}) copy-start(f32[256,16]{0,1:T(8,128)} %get-tuple-element.175) | copy-start | bytes 49156
  107.5 13.2 %copy-start.9 = (f32[256,16]{0,1:T(8,128)S(1)}, f32[256,16]{0,1:T(8,128)}, u32[]{:S(2)}) copy-start(f32[256,16]{0,1:T(8,128)} %get-tuple-element.176) | copy-start | bytes 49156
  107.5 13.2 %copy-start.10 = (f32[256,16]{0,1:T(8,128)S(1)}, f32[256,16]{0,1:T(8,128)}, u32[]{:S(2)}) copy-start(f32[256,16]{0,1:T(8,128)} %get-tuple-element.174) | copy-start | bytes 49156
  107.5 13.2 %copy-start.25 = (f32[16]{0:T(128)S(1)}, f32[16]{0:T(128)}, u32[]{:S(2)}) copy-start(f32[16]{0:T(128)} %param.22) | copy-start | bytes 196
  121.9 7.3 %copy-start.21 = (f32[1024]{0:T(1024)S(1)}, f32[1024]{0:T(1024)}, u32[]{:S(2)}) copy-start(f32[1024]{0:T(1024)} %get-tuple-element.169) | copy-start | bytes 12292
  121.9 8.1 %copy-start.4 = (bf16[256,1024]{1,0:T(8,128)(2,1)S(1)}, bf16[256,1024]{1,0:T(8,128)(2,1)}, u32[]{:S(2)}) copy-start(bf16[256,1024]{1,0:T(8,128)(2,1)} %get-tuple-element.170) | copy-start | bytes 1572868
  121.9 8.3 %copy-start.1 = (bf16[1,1024,128]{2,1,0:T(8,128)(2,1)S(1)}, bf16[1,1024,128]{2,1,0:T(8,128)(2,1)}, u32[]{:S(2)}) copy-start(bf16[1,1024,128]{2,1,0:T(8,128)(2,1)} %param.23) | copy-start | bytes 786436
  129.2 65.2 %reduce-scatter.5.cloned.1.call-start = ((), (), s32[]{:S(2)}) async-start(), calls=%async_computation.4 | async-start | bytes 163840 | tf_op jit(solution)/shard_map/reduce_scatter | solution.py:111
  130.8 3.8 %copy-start.6 = (f32[16,256]{1,0:T(8,128)S(1)}, f32[16,256]{1,0:T(8,128)}, u32[]{:S(2)}) copy-start(f32[16,256]{1,0:T(8,128)} %param.19) | copy-start | bytes 49156
  130.9 3.8 %copy-start.11 = (f32[256,16]{0,1:T(8,128)S(1)}, f32[256,16]{0,1:T(8,128)}, u32[]{:S(2)}) copy-start(f32[256,16]{0,1:T(8,128)} %get-tuple-element.152) | copy-start | bytes 49156
  130.9 3.8 %copy-start.17 = (f32[16,2]{0,1:T(2,128)S(1)}, f32[16,2]{0,1:T(2,128)}, u32[]{:S(2)}) copy-start(f32[16,2]{0,1:T(2,128)} %copy-done.16) | copy-start | bytes 388
  130.9 3.8 %copy-start.18 = (f32[16]{0:T(128)S(1)}, f32[16]{0:T(128)}, u32[]{:S(2)}) copy-start(f32[16]{0:T(128)} %param.20) | copy-start | bytes 196
  130.9 3.8 %copy-start.20 = (f32[16]{0:T(128)S(1)}, f32[16]{0:T(128)}, u32[]{:S(2)}) copy-start(f32[16]{0:T(128)} %copy-done.19) | copy-start | bytes 196
  130.9 4.4 %copy-start.14 = (f32[16,256]{1,0:T(8,128)S(1)}, f32[16,256]{1,0:T(8,128)}, u32[]{:S(2)}) copy-start(f32[16,256]{1,0:T(8,128)} %copy-done.13) | copy-start | bytes 49156
  130.9 5.8 %copy-start.8 = (f32[256,16]{0,1:T(8,128)S(1)}, f32[256,16]{0,1:T(8,128)}, u32[]{:S(2)}) copy-start(f32[256,16]{0,1:T(8,128)} %get-tuple-element.175) | copy-start | bytes 49156
  130.9 6.9 %copy-start.12 = (f32[256,16]{0,1:T(8,128)S(1)}, f32[256,16]{0,1:T(8,128)}, u32[]{:S(2)}) copy-start(f32[256,16]{0,1:T(8,128)} %get-tuple-element.153) | copy-start | bytes 49156
  130.9 6.9 %copy-start.23 = (f32[16]{0:T(128)S(1)}, f32[16]{0:T(128)}, u32[]{:S(2)}) copy-start(f32[16]{0:T(128)} %copy-done.22) | copy-start | bytes 196
  130.9 7.7 %copy-start.24 = (f32[16]{0:T(128)S(1)}, f32[16]{0:T(128)}, u32[]{:S(2)}) copy-start(f32[16]{0:T(128)} %reduce_sum.127) | copy-start | bytes 196
Sparse Core Ops, SparseCore 0:
  9.6 48.3 all-gather.4
  67.3 35.4 all-gather.6
  129.3 43.6 reduce-scatter.2
  175.7 18.6 reduce-scatter.4
where the time goes:
time: 202 us; the launch traced here: 201 us
  waiting for transfers between devices  102 us (50%)
  blocking collectives  27.8 us (14%)
  matrix products  24.4 us (12%)
  local copies, waits for them, and re-layouts  16.4 us (8%)
  other arithmetic  15.7 us (8%)
  between operations  14.7 us (7%)
    all_gather x1, waiting for transfers between devices, shards(): lax.all_gather(out_grad, 'head', axis=1, tiled=True)  45.1 us
    reduce_scatter x1, waiting for transfers between devices, shards(): lax.psum_scatter(lax.dot_general(w_in, x_grad, contract_last, preferred_e...  19.8 us
    reduce_scatter x1, waiting for transfers between devices, shards(): lax.psum_scatter(bc_part.astype(jnp.bfloat16), 'head', scatter_dimension=...  19.4 us
    all_gather x1, waiting for transfers between devices, entering(): pieces = jax.tree.map(lambda part: lax.all_gather(part, axis), value)  16.6 us
    unnamed x1, blocking collectives  13.9 us
    psum x1, blocking collectives, shards(): param_grad = lax.psum(param_terms, 'seq') * norm_scale  13.9 us
    select_n x7, other arithmetic, turn(): jnp.where(position < mine, new, old)  8.18 us
    dot_general x1, matrix products, shards(): lax.dot_general(lax.all_gather(out_grad, 'head', axis=1, tiled=True), w_o...  7.83 us
  transfers between devices with their start and end apart: 4, of which 4 were waited for; matrix products, arithmetic and copies ran while one was open for 10% of the time, Pallas kernels for 0%

commit v1 on v0

--- a/solution.py
+++ b/solution.py
@@ -2,6 +2,19 @@
 import jax.numpy as jnp
 from jax import lax
 from jax.sharding import PartitionSpec as P
+
+
+def gather_around(value, axis, dim):
+    ways = lax.axis_size(axis)
+    up = [(d, (d + 1) % ways) for d in range(ways)]
+    down = [(d, (d - 1) % ways) for d in range(ways)]
+    earlier, later = ([value], [value])
+    for _ in range(ways // 2):
+        earlier.append(lax.ppermute(earlier[-1], axis, up))
+    for _ in range((ways - 1) // 2):
+        later.append(lax.ppermute(later[-1], axis, down))
+    line = jnp.concatenate([*earlier[::-1], *later[1:]], axis=dim)
+    return jnp.roll(line, (lax.axis_index(axis) - ways // 2) * value.shape[dim], axis=dim)
 
 
 def entering(value, axis, join, neutral):
@@ -27,10 +40,7 @@
     state_dim = b_in.shape[1]
     contract_last = (((1,), (1,)), ((), ()))
     head_sum = lax.dot_general(
-        lax.all_gather(out_grad, "head", axis=1, tiled=True),
-        w_out,
-        contract_last,
-        preferred_element_type=jnp.float32,
+        gather_around(out_grad, "head", 1), w_out, contract_last, preferred_element_type=jnp.float32
     )
     dy_heads = head_sum.astype(jnp.bfloat16).reshape(tokens_here, group_heads, head_dim)
     dy_wide = dy_heads.astype(jnp.float32)

time: 202 us -> 192 us (0.950)
  waiting for transfers between devices: 102 us -> 87.1 us
  starting transfers between devices: 0.16 us -> 5.5 us
    all_gather x1 -> x0, waiting for transfers between devices: 45.1 us -> none  [shards(): lax.all_gather(out_grad, 'head', axis=1, tiled=True)]
    ppermute x0 -> x3, waiting for transfers between devices: none -> 29.2 us  [the longest x2 29.2 us: gather_around(): earlier.append(lax.ppermute(earlier[-1], axis, up))]
    ppermute x0 -> x3, starting transfers between devices: none -> 5.2 us  [the longest x2 3.11 us: gather_around(): earlier.append(lax.ppermute(earlier[-1], axis, up))]
    all_gather x1, waiting for transfers between devices: 16.6 us -> 18.8 us  [entering(): pieces = jax.tree.map(lambda part: lax.all_gather(part, axis), value)]
  transfers between devices with their start and end apart: 4 -> 6, of which waited for: 4 -> 5; matrix products, arithmetic and copies ran while one was open for 10% -> 11% of each run, Pallas kernels for 0% -> 0%
where the time goes in v1:
time: 192 us; the launch traced here: 190 us
  waiting for transfers between devices  87.1 us (45%)
  blocking collectives  26.2 us (14%)
  matrix products  23.8 us (12%)
  local copies, waits for them, and re-layouts  17.1 us (9%)
  other arithmetic  15.7 us (8%)
  between operations  14.8 us (8%)
  starting transfers between devices  5.5 us (3%)
    ppermute x2, waiting for transfers between devices, gather_around(): earlier.append(lax.ppermute(earlier[-1], axis, up))  29.2 us
    reduce_scatter x1, waiting for transfers between devices, shards(): lax.psum_scatter(lax.dot_general(w_in, x_grad, contract_last, preferred_e...  19.7 us
    reduce_scatter x1, waiting for transfers between devices, shards(): lax.psum_scatter(bc_part.astype(jnp.bfloat16), 'head', scatter_dimension=...  19.5 us
    all_gather x1, waiting for transfers between devices, entering(): pieces = jax.tree.map(lambda part: lax.all_gather(part, axis), value)  18.8 us
    psum x1, blocking collectives, shards(): param_grad = lax.psum(param_terms, 'seq') * norm_scale  13.9 us
    unnamed x1, blocking collectives  12.3 us
    select_n x7, other arithmetic, turn(): jnp.where(position < mine, new, old)  8.18 us
    dot_general x1, matrix products, shards(): lax.dot_general(gather_around(out_grad, 'head', 1), w_out, contract_last,...  7.29 us
  transfers between devices with their start and end apart: 6, of which 5 were waited for; matrix products, arithmetic and copies ran while one was open for 11% of the time, Pallas kernels for 0%

profile of v1, /device:TPU:0, one launch (start us, length us, event | category | flops | bytes accessed | tf_op | source)
XLA Modules:
  0.0 190.5 jit_solution(15319737084740426277)
XLA Ops:
  7.2 3.1 %collective-permute-start = (bf16[256,1024]{1,0:T(8,128)(2,1)}, bf16[256,1024]{1,0:T(8,128)(2,1)S(1)}, u32[]{:S(2)}, u32[]{:S(2)}) collective-permute-start(bf16[256,1024]{1,0:T(8,128)(2,1)} %param.15), channel_id=1, source_target_pairs={{0,1},{1,2},{2,3},{3,0},{4,5},{5,6},{6,7},{7,4},{8,9},{9,10},{10,1... | collective-permute-start | bytes 1572872 | tf_op jit(solution)/shard_map/ppermute | solution.py:13
  10.3 2.1 %collective-permute-start.2 = (bf16[256,1024]{1,0:T(8,128)(2,1)}, bf16[256,1024]{1,0:T(8,128)(2,1)S(1)}, u32[]{:S(2)}, u32[]{:S(2)}) collective-permute-start(bf16[256,1024]{1,0:T(8,128)(2,1)} %param.15), channel_id=1, source_target_pairs={{0,3},{1,0},{2,1},{3,2},{4,7},{5,4},{6,5},{7,6},{8,11},{9,8},{10,9... | collective-permute-start | bytes 1572872 | tf_op jit(solution)/shard_map/ppermute | solution.py:15
  12.4 0.7 exponential_negate_fusion
  13.1 0.8 copy_bitcast_fusion.3
  13.9 0.6 reduce-window.14
  14.7 10.7 %collective-permute-done = bf16[256,1024]{1,0:T(8,128)(2,1)S(1)} collective-permute-done((bf16[256,1024]{1,0:T(8,128)(2,1)}, bf16[256,1024]{1,0:T(8,128)(2,1)S(1)}, u32[]{:S(2)}, u32[]{:S(2)}) %collective-permute-start) | collective-permute-done | bytes 524320 | tf_op jit(solution)/shard_map/ppermute | solution.py:13
  25.7 1.4 fusion.40
  27.2 1.3 copy.72
  28.5 18.5 %collective-permute-done.1 = bf16[256,1024]{1,0:T(8,128)(2,1)S(1)} collective-permute-done((bf16[256,1024]{1,0:T(8,128)(2,1)S(1)}, bf16[256,1024]{1,0:T(8,128)(2,1)S(1)}, u32[]{:S(2)}, u32[]{:S(2)}) %collective-permute-start.1) | collective-permute-done | bytes 524320 | tf_op jit(solution)/shard_map/ppermute | solution.py:13
  47.5 7.3 %fusion.22 = (f32[1024]{0:T(1024)}, bf16[256,1024]{1,0:T(8,128)(2,1)}, bf16[256,1024]{1,0:T(8,128)(2,1)S(1)}) fusion(bf16[256,1024]{1,0:T(8,128)(2,1)S(1)} %copy-done.5, f32[256,1024]{1,0:T(8,128)S(1)} %copy-done.2, bf16[1024,4096]{1,0:T(8,128)(2,1)} %param.24, bf16[256,8192]{1,0:T(8,128)(2,1)S(1)} %constant_dynamic-update-slice_fusion, s32[]{:T(128)S(6)} %select_n.45), kind=kOutput, calls=%fused_computation.38 | convolution fusion | flops 2149317632 | bytes 13111300 | tf_op jit(solution)/shard_map/dot_general | solution.py:42
  55.0 1.1 fusion.27
  56.4 0.6 dynamic-slice.8
  57.8 12.3 %all-reduce = f32[128]{0:T(128)S(1)} all-reduce(f32[128]{0:T(128)S(1)} %dynamic-update-slice.3), channel_id=2, replica_groups=mesh['seq'=8,'head'=4] {'seq'}, use_global_device_ids=true, to_apply=%add | all-reduce | flops 128 | bytes 1024
  70.2 0.6 rev.12
  71.0 0.4 copy-done.18
  71.4 2.0 %fusion.12 = f32[256,16,64]{0,2,1:T(8,128)S(1)} fusion(bf16[256,16,64]{0,2,1:T(8,128)(2,1)S(1)} %bitcast.132, f32[16,256]{1,0:T(8,128)} %copy-done.16, f32[256,256]{1,0:T(8,128)S(1)} %fusion.50, pred[256,256]{1,0:T(8,128)(4,1)S(1)} %iota_compare_fusion), kind=kOutput, calls=%fused_computation.23 | convolution fusion | flops 139460608 | bytes 1916928 | tf_op jit(solution)/shard_map/hij,ihp->jhp/dot_general | solution.py:62
  73.4 18.8 %all-gather.4.cloned.1.call-done = f32[128,64,128]{2,1,0:T(8,128)} async-done(((f32[16,64,128]{2,1,0:T(8,128)}), f32[128,64,128]{2,1,0:T(8,128)}) %all-gather.4.cloned.1.call-update) | async-done | bytes 4194320 | tf_op jit(solution)/shard_map/all_gather | solution.py:22
  92.2 4.7 %rev.13 = f32[8,16,64,128]{3,2,1,0:T(8,128)} reverse(f32[8,16,64,128]{3,2,1,0:T(8,128)} %bitcast.135), dimensions={0} | reverse | bytes 8388608 | tf_op jit(solution)/shard_map/rev | solution.py:23
  96.9 13.2 %while.15 = (s32[]{:T(128)}, f32[16,64,128]{2,1,0:T(8,128)S(1)}, s32[]{:T(128)}, f32[8,16]{1,0:T(8,128)}, f32[8,16,64,128]{3,2,1,0:T(8,128)}, /*index=5*/s32[]{:T(128)}, s32[]{:T(128)}) while((s32[]{:T(128)}, f32[16,64,128]{2,1,0:T(8,128)S(1)}, s32[]{:T(128)}, f32[8,16]{1,0:T(8,128)}, f32[8,16,64,128]{3,2,1,0:T(8,128)}, ...), condition=%wide.region_3.4_spmd.clone, body=%wide.region_2.3_spmd.clone.sunk | while | flops 524292 | bytes 1573161 | solution.py:33
  96.9 0.7 dynamic-slice_bitcast_fusion.2
  97.7 1.2 fusion.67
  98.8 0.7 dynamic-slice_bitcast_fusion.2
  99.5 1.2 fusion.67
  100.7 0.7 dynamic-slice_bitcast_fusion.2
  101.4 1.2 fusion.67
  102.6 0.7 dynamic-slice_bitcast_fusion.2
  103.3 1.2 fusion.67
  104.5 0.7 dynamic-slice_bitcast_fusion.2
  105.2 1.2 fusion.67
  106.4 0.7 dynamic-slice_bitcast_fusion.2
  107.0 1.2 fusion.67
  108.2 0.7 dynamic-slice_bitcast_fusion.2
  108.9 1.2 fusion.67
  110.1 1.2 multiply_reduce_fusion.1
  111.4 7.2 %fusion.1 = bf16[4096,256]{0,1:T(8,128)(2,1)} fusion(bf16[256,1024]{0,1:T(8,128)(2,1)S(1)} %bitcast.141, bf16[4096,1024]{1,0:T(8,128)(2,1)} %param.25), kind=kOutput, calls=%fused_computation.4 | convolution fusion | flops 2148532224 | bytes 11010048 | tf_op jit(solution)/shard_map/dot_general | solution.py:114
  119.0 0.7 reduce_sum.127
  119.9 0.3 convolution_bitcast_fusion.1
  120.2 0.3 fusion.16
  120.6 3.5 %fusion.2 = (f32[16,256]{1,0:T(8,128)S(1)}, f32[16,256]{1,0:T(8,128)S(1)}, bf16[256,256]{1,0:T(8,128)(2,1)S(1)}) fusion(f32[16,256]{1,0:T(8,128)} %copy-done.16, f32[256,256]{1,0:T(8,128)} %copy-done.8, pred[256,256]{1,0:T(8,128)(4,1)} %copy-done.18, bf16[256,16,64]{0,2,1:T(8,128)(2,1)S(1)} %bitcast.134, f32[256,16,64]{0,2,1:T(8,128)S(1)} %bitcast.129, ...), kind=kOutput, calls=%fused_computation.10 | convolution fusion | flops 146202624 | bytes 2097152 | tf_op jit(solution)/shard_map/ihp,jhp->hij/dot_general | solution.py:60
  125.3 0.6 reduce-window.16
  126.3 0.3 convolution_bitcast_fusion.2
  126.8 0.7 pad_maximum_fusion
  127.4 0.8 fusion.48
  128.3 13.9 %psum.7 = f32[3,16]{1,0:T(4,128)S(1)} all-reduce(f32[3,16]{1,0:T(4,128)S(1)} %pad_maximum_fusion.1), channel_id=1, replica_groups=mesh['seq'=8,'head'=4] {'seq'}, use_global_device_ids=true, to_apply=%region_20.21 | all-reduce | flops 48 | bytes 384 | tf_op jit(solution)/shard_map/psum | solution.py:123
  142.2 0.6 broadcast_multiply_fusion
  142.8 19.7 %reduce-scatter.3.cloned.1.call-done = bf16[1024,256]{0,1:T(8,128)(2,1)} async-done(((bf16[4096,256]{0,1:T(8,128)(2,1)}), bf16[1024,256]{0,1:T(8,128)(2,1)}) %reduce-scatter.3.cloned.1.call-update) | async-done | bytes 524304 | tf_op jit(solution)/shard_map/reduce_scatter | solution.py:113
  162.4 2.0 %copy.78 = bf16[1024,256]{1,0:T(8,128)(2,1)} copy(bf16[1024,256]{0,1:T(8,128)(2,1)} %reduce-scatter.3.cloned.1.call-done) | data formatting | bytes 1048576
  164.5 19.5 %reduce-scatter.5.cloned.1.call-done = bf16[64,256]{1,0:T(8,128)(2,1)} async-done(((bf16[256,256]{1,0:T(8,128)(2,1)}), bf16[64,256]{1,0:T(8,128)(2,1)}) %reduce-scatter.5.cloned.1.call-update) | async-done | bytes 32784 | tf_op jit(solution)/shard_map/reduce_scatter | solution.py:121
  (107 shorter events, 4.3 us)
Async XLA Ops:
  7.2 63.6 %copy-start = (bf16[256,128]{1,0:T(8,128)(2,1)S(1)}, bf16[256,128]{1,0:T(8,128)(2,1)}, u32[]{:S(2)}) copy-start(bf16[256,128]{1,0:T(8,128)(2,1)} %param.17) | copy-start | bytes 196612
  7.2 39.9 %copy-start.1 = (bf16[256,1024]{1,0:T(8,128)(2,1)S(1)}, bf16[256,1024]{1,0:T(8,128)(2,1)}, u32[]{:S(2)}) copy-start(bf16[256,1024]{1,0:T(8,128)(2,1)} %param.15) | copy-start | bytes 1572868
  7.2 85.0 %all-gather.4.cloned.1.call-start = ((), (), s32[]{:S(2)}) async-start(), calls=%async_computation.4 | async-start | bytes 4718592 | tf_op jit(solution)/shard_map/all_gather | solution.py:22
  7.2 18.2 %collective-permute-start = (bf16[256,1024]{1,0:T(8,128)(2,1)}, bf16[256,1024]{1,0:T(8,128)(2,1)S(1)}, u32[]{:S(2)}, u32[]{:S(2)}) collective-permute-start(bf16[256,1024]{1,0:T(8,128)(2,1)} %param.15), channel_id=1, source_target_pairs={{0,1},{1,2},{2,3},{3,0},{4,5},{5,6},{6,7},{7,4},{8,9},{9,10},{10,1... | collective-permute-start | bytes 1572872 | tf_op jit(solution)/shard_map/ppermute | solution.py:13
  10.3 36.8 %collective-permute-start.2 = (bf16[256,1024]{1,0:T(8,128)(2,1)}, bf16[256,1024]{1,0:T(8,128)(2,1)S(1)}, u32[]{:S(2)}, u32[]{:S(2)}) collective-permute-start(bf16[256,1024]{1,0:T(8,128)(2,1)} %param.15), channel_id=1, source_target_pairs={{0,3},{1,0},{2,1},{3,2},{4,7},{5,4},{6,5},{7,6},{8,11},{9,8},{10,9... | collective-permute-start | bytes 1572872 | tf_op jit(solution)/shard_map/ppermute | solution.py:15
  13.1 1.6 copy-start.25
  14.7 32.6 %copy-start.19 = (f32[16,2]{0,1:T(2,128)}, f32[16,2]{0,1:T(2,128)S(1)}, u32[]{:S(2)}) copy-start(f32[16,2]{0,1:T(2,128)S(1)} %slice.34) | copy-start | bytes 388
  25.4 21.6 %collective-permute-start.1 = (bf16[256,1024]{1,0:T(8,128)(2,1)S(1)}, bf16[256,1024]{1,0:T(8,128)(2,1)S(1)}, u32[]{:S(2)}, u32[]{:S(2)}) collective-permute-start(bf16[256,1024]{1,0:T(8,128)(2,1)S(1)} %collective-permute-done), channel_id=1, source_target_pairs={{0,1},{1,2},{2,3},{3,0},{4,5},{5,6},{6,7},{7,4},{8,9},{9,10},{10,1... | collective-permute-start | bytes 1572872 | tf_op jit(solution)/shard_map/ppermute | solution.py:13
  25.5 21.8 %copy-start.16 = (f32[16,256]{1,0:T(8,128)}, f32[16,256]{1,0:T(8,128)S(1)}, u32[]{:S(2)}) copy-start(f32[16,256]{1,0:T(8,128)S(1)} %copy_bitcast_fusion.1) | copy-start | bytes 49156
  25.7 21.6 %copy-start.22 = (f32[16]{0:T(128)}, f32[16]{0:T(128)S(1)}, u32[]{:S(2)}) copy-start(f32[16]{0:T(128)S(1)} %get-tuple-element.154) | copy-start | bytes 196
  28.5 18.9 %copy-start.2 = (f32[256,1024]{1,0:T(8,128)S(1)}, f32[256,1024]{1,0:T(8,128)}, u32[]{:S(2)}) copy-start(f32[256,1024]{1,0:T(8,128)} %copy.72) | copy-start | bytes 3145732
  28.5 18.9 %copy-start.5 = (bf16[256,1024]{1,0:T(8,128)(2,1)S(1)}, bf16[256,1024]{1,0:T(8,128)(2,1)}, u32[]{:S(2)}) copy-start(bf16[256,1024]{1,0:T(8,128)(2,1)} %param.16) | copy-start | bytes 1572868
  47.4 7.5 %copy-start.4 = (bf16[256,128]{1,0:T(8,128)(2,1)S(1)}, bf16[256,128]{1,0:T(8,128)(2,1)}, u32[]{:S(2)}) copy-start(bf16[256,128]{1,0:T(8,128)(2,1)} %param.18) | copy-start | bytes 196612
  47.5 8.7 %copy-start.6 = (bf16[256,1024]{1,0:T(8,128)(2,1)S(1)}, bf16[256,1024]{1,0:T(8,128)(2,1)}, u32[]{:S(2)}) copy-start(bf16[256,1024]{1,0:T(8,128)(2,1)} %param.16) | copy-start | bytes 1572868
  54.8 1.6 copy-start.29
  56.1 106.3 %reduce-scatter.3.cloned.1.call-start = ((), (), s32[]{:S(2)}) async-start(), calls=%async_computation.2 | async-start | bytes 2621440 | tf_op jit(solution)/shard_map/reduce_scatter | solution.py:113
  70.8 0.6 copy-start.18
  71.4 25.5 %copy-start.8 = (f32[256,256]{1,0:T(8,128)}, f32[256,256]{1,0:T(8,128)S(1)}, u32[]{:S(2)}) copy-start(f32[256,256]{1,0:T(8,128)S(1)} %fusion.50) | copy-start | bytes 786436
  96.9 13.2 %copy-start.10 = (f32[256,16]{0,1:T(8,128)S(1)}, f32[256,16]{0,1:T(8,128)}, u32[]{:S(2)}) copy-start(f32[256,16]{0,1:T(8,128)} %get-tuple-element.175) | copy-start | bytes 49156
  96.9 13.2 %copy-start.12 = (f32[256,16]{0,1:T(8,128)S(1)}, f32[256,16]{0,1:T(8,128)}, u32[]{:S(2)}) copy-start(f32[256,16]{0,1:T(8,128)} %get-tuple-element.176) | copy-start | bytes 49156
  96.9 13.2 %copy-start.13 = (f32[256,16]{0,1:T(8,128)S(1)}, f32[256,16]{0,1:T(8,128)}, u32[]{:S(2)}) copy-start(f32[256,16]{0,1:T(8,128)} %get-tuple-element.174) | copy-start | bytes 49156
  96.9 13.2 %copy-start.28 = (f32[16]{0:T(128)S(1)}, f32[16]{0:T(128)}, u32[]{:S(2)}) copy-start(f32[16]{0:T(128)} %param.22) | copy-start | bytes 196
  111.4 7.5 %copy-start.24 = (f32[1024]{0:T(1024)S(1)}, f32[1024]{0:T(1024)}, u32[]{:S(2)}) copy-start(f32[1024]{0:T(1024)} %get-tuple-element.169) | copy-start | bytes 12292
  111.4 8.3 %copy-start.7 = (bf16[256,1024]{1,0:T(8,128)(2,1)S(1)}, bf16[256,1024]{1,0:T(8,128)(2,1)}, u32[]{:S(2)}) copy-start(bf16[256,1024]{1,0:T(8,128)(2,1)} %get-tuple-element.170) | copy-start | bytes 1572868
  111.4 8.5 %copy-start.3 = (bf16[1,1024,128]{2,1,0:T(8,128)(2,1)S(1)}, bf16[1,1024,128]{2,1,0:T(8,128)(2,1)}, u32[]{:S(2)}) copy-start(bf16[1,1024,128]{2,1,0:T(8,128)(2,1)} %param.23) | copy-start | bytes 786436
  118.6 65.3 %reduce-scatter.5.cloned.1.call-start = ((), (), s32[]{:S(2)}) async-start(), calls=%async_computation.3 | async-start | bytes 163840 | tf_op jit(solution)/shard_map/reduce_scatter | solution.py:121
  120.5 3.8 %copy-start.9 = (f32[16,256]{1,0:T(8,128)S(1)}, f32[16,256]{1,0:T(8,128)}, u32[]{:S(2)}) copy-start(f32[16,256]{1,0:T(8,128)} %param.19) | copy-start | bytes 49156
  120.5 3.8 %copy-start.14 = (f32[256,16]{0,1:T(8,128)S(1)}, f32[256,16]{0,1:T(8,128)}, u32[]{:S(2)}) copy-start(f32[256,16]{0,1:T(8,128)} %get-tuple-element.152) | copy-start | bytes 49156
  120.5 3.8 %copy-start.20 = (f32[16,2]{0,1:T(2,128)S(1)}, f32[16,2]{0,1:T(2,128)}, u32[]{:S(2)}) copy-start(f32[16,2]{0,1:T(2,128)} %copy-done.19) | copy-start | bytes 388
  120.5 3.8 %copy-start.21 = (f32[16]{0:T(128)S(1)}, f32[16]{0:T(128)}, u32[]{:S(2)}) copy-start(f32[16]{0:T(128)} %param.20) | copy-start | bytes 196
  120.5 3.8 %copy-start.23 = (f32[16]{0:T(128)S(1)}, f32[16]{0:T(128)}, u32[]{:S(2)}) copy-start(f32[16]{0:T(128)} %copy-done.22) | copy-start | bytes 196
  120.5 4.4 %copy-start.17 = (f32[16,256]{1,0:T(8,128)S(1)}, f32[16,256]{1,0:T(8,128)}, u32[]{:S(2)}) copy-start(f32[16,256]{1,0:T(8,128)} %copy-done.16) | copy-start | bytes 49156
  120.5 5.8 %copy-start.11 = (f32[256,16]{0,1:T(8,128)S(1)}, f32[256,16]{0,1:T(8,128)}, u32[]{:S(2)}) copy-start(f32[256,16]{0,1:T(8,128)} %get-tuple-element.175) | copy-start | bytes 49156
  120.5 6.9 %copy-start.15 = (f32[256,16]{0,1:T(8,128)S(1)}, f32[256,16]{0,1:T(8,128)}, u32[]{:S(2)}) copy-start(f32[256,16]{0,1:T(8,128)} %get-tuple-element.153) | copy-start | bytes 49156
  120.5 6.9 %copy-start.26 = (f32[16]{0:T(128)S(1)}, f32[16]{0:T(128)}, u32[]{:S(2)}) copy-start(f32[16]{0:T(128)} %copy-done.25) | copy-start | bytes 196
  120.6 7.7 %copy-start.27 = (f32[16]{0:T(128)S(1)}, f32[16]{0:T(128)}, u32[]{:S(2)}) copy-start(f32[16]{0:T(128)} %reduce_sum.127) | copy-start | bytes 196
Sparse Core Ops, SparseCore 0:
  56.2 35.9 all-gather.3
  118.8 43.6 reduce-scatter.2
  165.3 18.6 reduce-scatter.4
